TPU v7x, 32 devices: a whole 2x2x4 slice. The times are simulated.
32 devices in a mesh: image: 2 (over x), row: 16 (over z, y, core).
Axes of the slice: x: 2, y: 2, z: 4, core: 2. Of those that a mesh axis runs over, the one named last changes fastest.
Arguments:
- density: float32 [256, 7, 128, 128], P(('image', 'row')), parts along dimension 0, as said below
- block_columns: int32 [256, 7], P(('image', 'row')), parts along dimension 0, may hold values from -1 to 127, as said below
Outputs:
- purified: float32 [256, 7, 128, 128], P(('image', 'row')), parts along dimension 0
- occupation: float32 [6], P('image'), parts along dimension 0
There are 2 independent parts, one for each index of `image`. A program takes and returns all parts, laid end to end along the dimension named above; each array names one. Nothing has to cross between parts.
Inputs may be any that keep to these rules, and one draw needn't show every extreme that they name: `block_columns`: slot s of block row i holds block column i - 3 + s or is empty (-1); slot 3 (column i) is never empty, and no slot points outside the matrix; the pattern is symmetric (j is in row i exactly when i is in row j); every draw has rows with all 7 slots filled. The density matrix is symmetric: the block in slot s of row i is the transpose of the block of row j = block_columns[i, s] whose column is i, and every diagonal block is symmetric.
All inputs are finite; a program needn't handle non-finite values.
Results may differ from a plain program's by a relative error of at most 0.0003.
Values sent between devices are 32-bit elements; how exact they have to be, the bound alone decides.
A program may use at most 128 MiB of HBM per device.

v0:
```python
import functools

import jax
import jax.numpy as jnp
from jax import lax
from jax.experimental import pallas as pl
from jax.experimental.pallas import tpu as pltpu
from jax.sharding import PartitionSpec as P

STEPS = 2
MESH = pl.DeviceIdType.MESH


def split(x):
    hi = x.astype(jnp.bfloat16)
    return hi, (x - hi.astype(jnp.float32)).astype(jnp.bfloat16)


def dot(a, b):
    return jnp.dot(a, b, preferred_element_type=jnp.float32)


def kernel(n, dens, cols, out, occ, pf, qf, sf, left, cube_left, rq_hi, rq_lo, rz_hi, rz_lo, mask,
           low0, up0, low1, up1, tr, trs, send, recv, tsend, trecv):
    rows, slots, bs, _ = dens.shape
    pairs = rows // 2
    me = lax.axis_index("row")
    f32 = jnp.float32

    barrier = pltpu.get_barrier_semaphore()

    @pl.loop(1, n)
    def _(k):
        pl.semaphore_signal(barrier, inc=1, device_id={"row": lax.rem(me + k, n)}, device_id_type=MESH)

    def blk(i):
        return slice(i * bs, (i + 1) * bs)

    def put_right(p, rb, col, hi, lo):
        q = p + (col + 1) // 2
        row, half = 3 + rb - 2 * ((col - 1) // 2) + 2, (col - 1) % 2
        rq_hi[q, blk(row), blk(half)] = hi
        rq_lo[q, blk(row), blk(half)] = lo
        if col % 2 == 0 and 0 <= 3 + rb - col <= 3:
            z, row, half = p + 2 + col // 2, 3 + rb - col, 0
        elif col % 2 == 1 and 0 <= rb + 6 - col <= 3:
            z, row, half = p + 2 + (col - 7) // 2, rb + 6 - col, 1
        else:
            return
        rz_hi[z, blk(row), blk(half)] = hi
        rz_lo[z, blk(row), blk(half)] = lo

    def put_halo(j, c, x):
        hi, lo = split(x)
        q = (c - 1) // 2
        row = j - (2 * q - 2)
        if 0 <= row <= 7:
            rq_hi[q + 1, blk(row), blk((c - 1) % 2)] = hi
            rq_lo[q + 1, blk(row), blk((c - 1) % 2)] = lo
        if c % 2 == 0 and 0 <= j - c <= 3 and c < rows:
            rz_hi[c // 2 + 2, blk(j - c), blk(0)] = hi
            rz_lo[c // 2 + 2, blk(j - c), blk(0)] = lo
        if c % 2 == 1 and 0 <= j - (c - 3) <= 3 and 7 <= c < rows + 7:
            z = (c - 7) // 2 + 2
            rz_hi[z, blk(j - c + 3), blk(1)] = hi
            rz_lo[z, blk(j - c + 3), blk(1)] = lo

    def put_left(ref, p, rb, col, hi, lo):
        ref[p, blk(rb), blk(col)] = hi
        ref[p, blk(2 + rb), blk(col)] = lo

    rq_hi[...] = jnp.zeros_like(rq_hi)
    rq_lo[...] = jnp.zeros_like(rq_lo)
    rz_hi[...] = jnp.zeros_like(rz_hi)
    rz_lo[...] = jnp.zeros_like(rz_lo)
    mask[...] = jnp.zeros_like(mask)
    trs[...] = jnp.zeros_like(trs)
    eye = (lax.broadcasted_iota(jnp.int32, (bs, bs), 0) == lax.broadcasted_iota(jnp.int32, (bs, bs), 1)).astype(f32)

    def diag(x):
        return jnp.sum(x * eye, axis=0, keepdims=True)

    def load(p, total):
        zero = jnp.zeros((bs, bs), jnp.bfloat16)
        for rb in range(2):
            for s in range(slots):
                col = s + rb
                m = (cols[2 * p + rb, s] >= 0).astype(f32)
                mask[p, rb : rb + 1, blk(col)] = jnp.full((1, bs), 1.0, f32) * m
                x = dens[2 * p + rb, s] * m
                pf[p, blk(rb), blk(col)] = x
                hi, lo = split(x)
                put_left(left, p, rb, col, hi, lo)
                put_right(p, rb, col, hi, lo)
                if s == slots // 2:
                    total = total + diag(x)
            put_left(left, p, rb, 7 - 7 * rb, zero, zero)
        return total

    trs[0:1, :] = lax.fori_loop(0, pairs, load, jnp.zeros((1, bs), f32))

    pl.semaphore_wait(barrier, n - 1)
    top = rows + 3

    def halo_copies(src, low, up, first):
        nxt, prv = [], []
        for h in range(3):
            e = rows + h
            p, rb = divmod(e - 3, 2)
            c0, c1 = (e, rows + 3) if first else (rows, e + 4)
            nxt.append((src.at[p, blk(rb), pl.ds((c0 - 2 * p) * bs, (c1 - c0) * bs)], low[h]))
            e = 3 + h
            p, rb = divmod(e - 3, 2)
            c0, c1 = (e, 6) if first else (e - 3, 6)
            prv.append((src.at[p, blk(rb), pl.ds((c0 - 2 * p) * bs, (c1 - c0) * bs)], up[h]))
        base = 0 if first else 6

        def make(pairs_, off, dev):
            return [
                pltpu.make_async_remote_copy(
                    src_ref=s, dst_ref=d, send_sem=send.at[base + off + k], recv_sem=recv.at[base + off + k],
                    device_id={"row": dev}, device_id_type=MESH)
                for k, (s, d) in enumerate(pairs_)
            ]

        return make(nxt, 0, lax.rem(me + 1, n)), make(prv, 3, lax.rem(me + n - 1, n))

    def start(copies):
        nxt, prv = copies

        @pl.when(me < n - 1)
        def _():
            for c in nxt:
                c.start()

        @pl.when(me > 0)
        def _():
            for c in prv:
                c.start()

    def wait_sends(copies):
        nxt, prv = copies

        @pl.when(me < n - 1)
        def _():
            for c in nxt:
                c.wait_send()

        @pl.when(me > 0)
        def _():
            for c in prv:
                c.wait_send()

    first = halo_copies(pf, low0, up0, True)
    start(first)

    def own0(e, c):
        p, rb = divmod(e - 3, 2)
        return pf[p, blk(rb), blk(c - 2 * p)]

    for j in list(range(3)) + list(range(top, top + 3)):
        for c in range(max(3, j - 3), min(top, j + 4)):
            put_halo(j, c, own0(c, j).T)

    @pl.when(me > 0)
    def _():
        for h in range(3):
            first[0][h].wait_recv()
        for h in range(3):
            for c in range(h, 3):
                x = low0[h][:, blk(c - h)]
                put_halo(h, c, x)
                if c > h:
                    put_halo(c, h, x.T)

    @pl.when(me < n - 1)
    def _():
        for h in range(3):
            first[1][h].wait_recv()
        for h in range(3):
            for c in range(h, 3):
                x = up0[h][:, blk(c - h)]
                put_halo(top + h, top + c, x)
                if c > h:
                    put_halo(top + c, top + h, x.T)

    def groups(ref, p):
        for g, (k0, k1, b0) in enumerate(((0, 6, 2), (0, 8, 0), (2, 8, 0))):
            a = ref[p, :, k0 * bs : k1 * bs]
            b = slice(b0 * bs, (b0 + k1 - k0) * bs)
            y = dot(a, rq_hi[p + g + 1, b, :])
            y = y[: 2 * bs] + y[2 * bs :] + dot(a[: 2 * bs], rq_lo[p + g + 1, b, :])
            for rb in range(2):
                for h in range(2):
                    yield rb, 1 + 2 * g + h, y[blk(rb), blk(h)]
        a = jnp.concatenate([ref[p, blk(r), (r % 2) * 4 * bs : (r % 2 + 1) * 4 * bs] for r in range(4)], axis=0)
        y = dot(a, rz_hi[p + 2])
        y = y[: 2 * bs] + y[2 * bs :] + dot(a[: 2 * bs], rz_lo[p + 2])
        yield 0, 0, y[blk(0), blk(0)]
        yield 1, 7, y[blk(1), blk(1)]

    def square(p, carry):
        for rb, col, y in groups(left, p):
            y = y * mask[p, rb : rb + 1, blk(col)]
            sf[p, blk(rb), blk(col)] = y
            put_left(cube_left, p, rb, col, *split(y))
        return carry

    zero = jnp.zeros((bs, bs), jnp.bfloat16)
    for p in range(pairs):
        for rb in range(2):
            put_left(cube_left, p, rb, 7 - 7 * rb, zero, zero)

    lax.fori_loop(0, pairs, square, 0)

    def cube(p, total):
        for rb, col, y in groups(cube_left, p):
            x = 3.0 * sf[p, blk(rb), blk(col)] - 2.0 * (y * mask[p, rb : rb + 1, blk(col)])
            qf[p, blk(rb), blk(col)] = x
            put_left(left, p, rb, col, *split(x))
            if col == 3 + rb:
                total = total + diag(x)
        return total

    trs[1:2, :] = lax.fori_loop(0, pairs, cube, jnp.zeros((1, bs), f32))

    second = halo_copies(qf, low1, up1, False)
    start(second)

    def refill(p, carry):
        for rb in range(2):
            for s in range(slots):
                col = s + rb
                put_right(p, rb, col, left[p, blk(rb), blk(col)], left[p, blk(2 + rb), blk(col)])
        return carry

    lax.fori_loop(0, pairs, refill, 0)

    @pl.when(me > 0)
    def _():
        for h in range(3):
            second[0][h].wait_recv()
        for h in range(3):
            for c in range(h + 4):
                put_halo(h, c, low1[h][:, blk(c)])

    @pl.when(me < n - 1)
    def _():
        for h in range(3):
            second[1][h].wait_recv()
        for h in range(3):
            for c in range(rows + h, top + 3):
                put_halo(top + h, c, up1[h][:, blk(c - rows - h)])

    lax.fori_loop(0, pairs, square, 0)

    def last(p, total):
        for rb, col, y in groups(cube_left, p):
            x = 3.0 * sf[p, blk(rb), blk(col)] - 2.0 * (y * mask[p, rb : rb + 1, blk(col)])
            out[2 * p + rb, col - rb] = x
            if col == 3 + rb:
                total = total + diag(x)
        return total

    trs[2:3, :] = lax.fori_loop(0, pairs, last, jnp.zeros((1, bs), f32))

    def trace_copy(k):
        return pltpu.make_async_remote_copy(
            src_ref=trs, dst_ref=tr.at[me], send_sem=tsend.at[k], recv_sem=trecv.at[k],
            device_id={"row": lax.rem(me + k, n)}, device_id_type=MESH)

    wait_sends(first)
    wait_sends(second)

    @pl.loop(1, n)
    def _(k):
        trace_copy(k).start()

    tr[me] = trs[...]

    @pl.loop(1, n)
    def _(k):
        trace_copy(k).wait()

    total = lax.fori_loop(0, n, lambda k, t: t + tr[k], jnp.zeros((8, bs), f32))
    for k in range(STEPS + 1):
        occ[k] = jnp.sum(total[k : k + 1, :]) / (n * rows * bs)


def on_device(density, block_columns):
    rows, slots, bs, _ = density.shape
    n = lax.axis_size("row")
    pairs = rows // 2
    f32, bf16 = jnp.float32, jnp.bfloat16
    vm = pltpu.VMEM
    wide = 8 * bs
    return pl.pallas_call(
        functools.partial(kernel, n),
        out_shape=(jax.ShapeDtypeStruct(density.shape, f32), jax.ShapeDtypeStruct((STEPS + 1,), f32)),
        in_specs=[pl.BlockSpec(memory_space=pltpu.VMEM), pl.BlockSpec(memory_space=pltpu.SMEM)],
        out_specs=(pl.BlockSpec(memory_space=pltpu.VMEM), pl.BlockSpec(memory_space=pltpu.SMEM)),
        scratch_shapes=[
            vm((pairs, 2 * bs, wide), f32),
            vm((pairs, 2 * bs, wide), f32),
            vm((pairs, 2 * bs, wide), f32),
            vm((pairs, 4 * bs, wide), bf16),
            vm((pairs, 4 * bs, wide), bf16),
            vm((pairs + 4, wide, 2 * bs), bf16),
            vm((pairs + 4, wide, 2 * bs), bf16),
            vm((pairs + 4, 4 * bs, 2 * bs), bf16),
            vm((pairs + 4, 4 * bs, 2 * bs), bf16),
            vm((pairs, 8, wide), f32),
            [vm((bs, (3 - h) * bs), f32) for h in range(3)],
            [vm((bs, (3 - h) * bs), f32) for h in range(3)],
            [vm((bs, (4 + h) * bs), f32) for h in range(3)],
            [vm((bs, (6 - h) * bs), f32) for h in range(3)],
            vm((n, 8, bs), f32),
            vm((8, bs), f32),
            pltpu.SemaphoreType.DMA((12,)),
            pltpu.SemaphoreType.DMA((12,)),
            pltpu.SemaphoreType.DMA((n,)),
            pltpu.SemaphoreType.DMA((n,)),
        ],
        compiler_params=pltpu.CompilerParams(collective_id=0, has_side_effects=True, vmem_limit_bytes=60 << 20),
    )(density, block_columns)


def solution(mesh):
    in_specs = (P(("image", "row"), None, None, None), P(("image", "row"), None))
    out_specs = (P(("image", "row"), None, None, None), P("image"))
    return jax.shard_map(on_device, mesh=mesh, in_specs=in_specs, out_specs=out_specs, check_vma=False)
```

profile of v0, /device:TPU:0, one launch (start us, length us, event | category | flops | bytes accessed | tf_op | source)
XLA Modules:
  0.0 73.6 jit_solution(16118846510696661642)
XLA Ops:
  0.6 68.1 %shard_map.41 = (f32[8,7,128,128]{3,2,1,0:T(8,128)}, f32[3]{0:T(128)}) custom-call(f32[8,7,128,128]{3,2,1,0:T(8,128)} %dens.1, s32[8,7]{1,0:T(8,128)} %cols.1), custom_call_target="tpu_custom_call" | custom-call | tf_op jit(solution)/shard_map/pallas_call | solution.py:297
  68.7 0.0 copy-start
  68.8 4.3 %copy.6 = f32[8,7,128,128]{3,2,1,0:T(8,128)} copy(f32[8,7,128,128]{3,2,1,0:T(8,128)} %get-tuple-element.4) | data formatting | bytes 7340032
  73.1 0.0 copy-done
  73.1 0.5 copy.7
Async XLA Ops:
  68.7 4.3 %copy-start = (f32[3]{0:T(128)S(1)}, f32[3]{0:T(128)}, u32[]{:S(2)}) copy-start(f32[3]{0:T(128)} %get-tuple-element.5) | copy-start | bytes 40
where the time goes:
time: 73.7 us; the launch traced here: 73.6 us
  Pallas kernels  68.1 us (92%)
  local copies, waits for them, and re-layouts  4.82 us (7%)
    pallas_call x1, Pallas kernels, on_device(): pl.pallas_call(functools.partial(kernel, n), out_shape=(jax.ShapeDtypeStr...  68.1 us
    unnamed x4, local copies, waits for them, and re-layouts  4.82 us

commit v1 on v0

--- a/solution.py
+++ b/solution.py
@@ -21,11 +21,17 @@
 
 
 def kernel(n, dens, cols, out, occ, pf, qf, sf, left, cube_left, rq_hi, rq_lo, rz_hi, rz_lo, mask,
-           low0, up0, low1, up1, tr, trs, send, recv, tsend, trecv):
+           low0, up0, low1, up1, tr, trs, buf, send, recv, tsend, trecv, isem, osem):
     rows, slots, bs, _ = dens.shape
     pairs = rows // 2
     me = lax.axis_index("row")
     f32 = jnp.float32
+
+    def fetch(p):
+        return pltpu.make_async_copy(dens.at[pl.ds(2 * p, 2)], buf.at[pl.ds(2 * p, 2)], isem.at[p])
+
+    for p in range(pairs):
+        fetch(p).start()
 
     barrier = pltpu.get_barrier_semaphore()
 
@@ -82,12 +88,13 @@
 
     def load(p, total):
         zero = jnp.zeros((bs, bs), jnp.bfloat16)
+        fetch(p).wait()
         for rb in range(2):
             for s in range(slots):
                 col = s + rb
                 m = (cols[2 * p + rb, s] >= 0).astype(f32)
                 mask[p, rb : rb + 1, blk(col)] = jnp.full((1, bs), 1.0, f32) * m
-                x = dens[2 * p + rb, s] * m
+                x = buf[2 * p + rb, s] * m
                 pf[p, blk(rb), blk(col)] = x
                 hi, lo = split(x)
                 put_left(left, p, rb, col, hi, lo)
@@ -154,6 +161,71 @@
     first = halo_copies(pf, low0, up0, True)
     start(first)
 
+    def triple(a, b_hi, b_lo):
+        y = dot(a, b_hi)
+        return y[: 2 * bs] + y[2 * bs :] + dot(a[: 2 * bs], b_lo)
+
+    spans = ((0, 6, 2), (0, 8, 0), (2, 8, 0))
+
+    def part(ref, p, g, k0, k1):
+        b0 = spans[g][2] - spans[g][0]
+        b = slice((b0 + k0) * bs, (b0 + k1) * bs)
+        return triple(ref[p, :, k0 * bs : k1 * bs], rq_hi[p + g + 1, b, :], rq_lo[p + g + 1, b, :])
+
+    def blocks(g, y):
+        for rb in range(2):
+            for h in range(2):
+                yield rb, 1 + 2 * g + h, y[blk(rb), blk(h)]
+
+    def corners(ref, p):
+        a = jnp.concatenate([ref[p, blk(r), (r % 2) * 4 * bs : (r % 2 + 1) * 4 * bs] for r in range(4)], axis=0)
+        y = triple(a, rz_hi[p + 2], rz_lo[p + 2])
+        yield 0, 0, y[blk(0), blk(0)]
+        yield 1, 7, y[blk(1), blk(1)]
+
+    def groups(ref, p, which=(0, 1, 2), corner=True):
+        for g in which:
+            yield from blocks(g, part(ref, p, g, *spans[g][:2]))
+        if corner:
+            yield from corners(ref, p)
+
+    def inner(p):
+        lo, hi = max(0, 3 - 2 * p), min(8, rows + 3 - 2 * p)
+        return lo + lo % 2, hi - hi % 2
+
+    def square_inner():
+        for p in range(pairs):
+            lo, hi = inner(p)
+            for g in range(3):
+                k0, k1 = max(lo, spans[g][0]), min(hi, spans[g][1])
+                sf[p, :, (1 + 2 * g) * bs : (3 + 2 * g) * bs] = part(left, p, g, k0, k1)
+
+    def square_outer():
+        for p in range(pairs):
+            lo, hi = inner(p)
+            for g in range(3):
+                y = sf[p, :, (1 + 2 * g) * bs : (3 + 2 * g) * bs]
+                if lo > spans[g][0]:
+                    y = y + part(left, p, g, spans[g][0], lo)
+                if hi < spans[g][1]:
+                    y = y + part(left, p, g, hi, spans[g][1])
+                for rb, col, x in blocks(g, y):
+                    put_square(p, rb, col, x)
+            for rb, col, x in corners(left, p):
+                put_square(p, rb, col, x)
+
+    def put_square(p, rb, col, y):
+        y = y * mask[p, rb : rb + 1, blk(col)]
+        sf[p, blk(rb), blk(col)] = y
+        put_left(cube_left, p, rb, col, *split(y))
+
+    zero = jnp.zeros((bs, bs), jnp.bfloat16)
+    for p in range(pairs):
+        for rb in range(2):
+            put_left(cube_left, p, rb, 7 - 7 * rb, zero, zero)
+
+    square_inner()
+
     def own0(e, c):
         p, rb = divmod(e - 3, 2)
         return pf[p, blk(rb), blk(c - 2 * p)]
@@ -184,34 +256,7 @@
                 if c > h:
                     put_halo(top + c, top + h, x.T)
 
-    def groups(ref, p):
-        for g, (k0, k1, b0) in enumerate(((0, 6, 2), (0, 8, 0), (2, 8, 0))):
-            a = ref[p, :, k0 * bs : k1 * bs]
-            b = slice(b0 * bs, (b0 + k1 - k0) * bs)
-            y = dot(a, rq_hi[p + g + 1, b, :])
-            y = y[: 2 * bs] + y[2 * bs :] + dot(a[: 2 * bs], rq_lo[p + g + 1, b, :])
-            for rb in range(2):
-                for h in range(2):
-                    yield rb, 1 + 2 * g + h, y[blk(rb), blk(h)]
-        a = jnp.concatenate([ref[p, blk(r), (r % 2) * 4 * bs : (r % 2 + 1) * 4 * bs] for r in range(4)], axis=0)
-        y = dot(a, rz_hi[p + 2])
-        y = y[: 2 * bs] + y[2 * bs :] + dot(a[: 2 * bs], rz_lo[p + 2])
-        yield 0, 0, y[blk(0), blk(0)]
-        yield 1, 7, y[blk(1), blk(1)]
-
-    def square(p, carry):
-        for rb, col, y in groups(left, p):
-            y = y * mask[p, rb : rb + 1, blk(col)]
-            sf[p, blk(rb), blk(col)] = y
-            put_left(cube_left, p, rb, col, *split(y))
-        return carry
-
-    zero = jnp.zeros((bs, bs), jnp.bfloat16)
-    for p in range(pairs):
-        for rb in range(2):
-            put_left(cube_left, p, rb, 7 - 7 * rb, zero, zero)
-
-    lax.fori_loop(0, pairs, square, 0)
+    square_outer()
 
     def cube(p, total):
         for rb, col, y in groups(cube_left, p):
@@ -222,10 +267,10 @@
                 total = total + diag(x)
         return total
 
-    trs[1:2, :] = lax.fori_loop(0, pairs, cube, jnp.zeros((1, bs), f32))
-
     second = halo_copies(qf, low1, up1, False)
-    start(second)
+    traced = cube(pairs - 1, cube(0, jnp.zeros((1, bs), f32)))
+    start((second[0][1:], second[1][:2]))
+    trs[1:2, :] = lax.fori_loop(1, pairs - 1, cube, traced)
 
     def refill(p, carry):
         for rb in range(2):
@@ -235,6 +280,8 @@
         return carry
 
     lax.fori_loop(0, pairs, refill, 0)
+    start((second[0][:1], second[1][2:]))
+    square_inner()
 
     @pl.when(me > 0)
     def _():
@@ -252,23 +299,33 @@
             for c in range(rows + h, top + 3):
                 put_halo(top + h, c, up1[h][:, blk(c - rows - h)])
 
-    lax.fori_loop(0, pairs, square, 0)
+    square_outer()
+
+    def put_out(p, rb, col, y):
+        x = 3.0 * sf[p, blk(rb), blk(col)] - 2.0 * (y * mask[p, rb : rb + 1, blk(col)])
+        buf[2 * p + rb, col - rb] = x
+        return x
 
     def last(p, total):
-        for rb, col, y in groups(cube_left, p):
-            x = 3.0 * sf[p, blk(rb), blk(col)] - 2.0 * (y * mask[p, rb : rb + 1, blk(col)])
-            out[2 * p + rb, col - rb] = x
+        for rb, col, y in groups(cube_left, p, (1,), False):
+            x = put_out(p, rb, col, y)
             if col == 3 + rb:
                 total = total + diag(x)
         return total
 
     trs[2:3, :] = lax.fori_loop(0, pairs, last, jnp.zeros((1, bs), f32))
+
+    def rest(p, carry):
+        for rb, col, y in groups(cube_left, p, (0, 2)):
+            put_out(p, rb, col, y)
+        return carry
 
     def trace_copy(k):
         return pltpu.make_async_remote_copy(
             src_ref=trs, dst_ref=tr.at[me], send_sem=tsend.at[k], recv_sem=trecv.at[k],
             device_id={"row": lax.rem(me + k, n)}, device_id_type=MESH)
 
+    tr[me] = trs[...]
     wait_sends(first)
     wait_sends(second)
 
@@ -276,7 +333,12 @@
     def _(k):
         trace_copy(k).start()
 
-    tr[me] = trs[...]
+    def store(p):
+        return pltpu.make_async_copy(buf.at[pl.ds(2 * p, 2)], out.at[pl.ds(2 * p, 2)], osem.at[p])
+
+    for p in range(pairs):
+        rest(p, 0)
+        store(p).start()
 
     @pl.loop(1, n)
     def _(k):
@@ -285,6 +347,8 @@
     total = lax.fori_loop(0, n, lambda k, t: t + tr[k], jnp.zeros((8, bs), f32))
     for k in range(STEPS + 1):
         occ[k] = jnp.sum(total[k : k + 1, :]) / (n * rows * bs)
+    for p in range(pairs):
+        store(p).wait()
 
 
 def on_device(density, block_columns):
@@ -297,8 +361,8 @@
     return pl.pallas_call(
         functools.partial(kernel, n),
         out_shape=(jax.ShapeDtypeStruct(density.shape, f32), jax.ShapeDtypeStruct((STEPS + 1,), f32)),
-        in_specs=[pl.BlockSpec(memory_space=pltpu.VMEM), pl.BlockSpec(memory_space=pltpu.SMEM)],
-        out_specs=(pl.BlockSpec(memory_space=pltpu.VMEM), pl.BlockSpec(memory_space=pltpu.SMEM)),
+        in_specs=[pl.BlockSpec(memory_space=pl.ANY), pl.BlockSpec(memory_space=pltpu.SMEM)],
+        out_specs=(pl.BlockSpec(memory_space=pl.ANY), pl.BlockSpec(memory_space=pltpu.SMEM)),
         scratch_shapes=[
             vm((pairs, 2 * bs, wide), f32),
             vm((pairs, 2 * bs, wide), f32),
@@ -316,10 +380,13 @@
             [vm((bs, (6 - h) * bs), f32) for h in range(3)],
             vm((n, 8, bs), f32),
             vm((8, bs), f32),
+            vm(density.shape, f32),
             pltpu.SemaphoreType.DMA((12,)),
             pltpu.SemaphoreType.DMA((12,)),
             pltpu.SemaphoreType.DMA((n,)),
             pltpu.SemaphoreType.DMA((n,)),
+            pltpu.SemaphoreType.DMA((pairs,)),
+            pltpu.SemaphoreType.DMA((pairs,)),
         ],
         compiler_params=pltpu.CompilerParams(collective_id=0, has_side_effects=True, vmem_limit_bytes=60 << 20),
     )(density, block_columns)

time: 73.7 us -> 59.5 us (0.81)
  Pallas kernels: 68.1 us -> 53.8 us
    pallas_call x1, Pallas kernels: 68.1 us -> 53.8 us  [on_device(): pl.pallas_call(functools.partial(kernel, n), out_shape=(jax.ShapeDtypeStr...]
where the time goes in v1:
time: 59.5 us; the launch traced here: 59.3 us
  Pallas kernels  53.8 us (90%)
  local copies, waits for them, and re-layouts  4.82 us (8%)
  between operations  0.65 us (1%)
    pallas_call x1, Pallas kernels, on_device(): pl.pallas_call(functools.partial(kernel, n), out_shape=(jax.ShapeDtypeStr...  53.8 us
    unnamed x4, local copies, waits for them, and re-layouts  4.82 us

profile of v1, /device:TPU:0, one launch (start us, length us, event | category | flops | bytes accessed | tf_op | source)
XLA Modules:
  0.0 59.3 jit_solution(8927065414666196327)
XLA Ops:
  0.6 53.8 %shard_map.41 = (f32[8,7,128,128]{3,2,1,0:T(8,128)}, f32[3]{0:T(128)}) custom-call(f32[8,7,128,128]{3,2,1,0:T(8,128)} %dens.1, s32[8,7]{1,0:T(8,128)} %cols.1), custom_call_target="tpu_custom_call" | custom-call | tf_op jit(solution)/shard_map/pallas_call | solution.py:361
  54.5 0.0 copy-start
  54.5 4.3 %copy.6 = f32[8,7,128,128]{3,2,1,0:T(8,128)} copy(f32[8,7,128,128]{3,2,1,0:T(8,128)} %get-tuple-element.4) | data formatting | bytes 7340032
  58.8 0.0 copy-done
  58.8 0.5 copy.7
Async XLA Ops:
  54.5 4.3 %copy-start = (f32[3]{0:T(128)S(1)}, f32[3]{0:T(128)}, u32[]{:S(2)}) copy-start(f32[3]{0:T(128)} %get-tuple-element.5) | copy-start | bytes 40

commit v2 on v1

--- a/solution.py
+++ b/solution.py
@@ -21,7 +21,7 @@
 
 
 def kernel(n, dens, cols, out, occ, pf, qf, sf, left, cube_left, rq_hi, rq_lo, rz_hi, rz_lo, mask,
-           low0, up0, low1, up1, tr, trs, buf, send, recv, tsend, trecv, isem, osem):
+           low0, up0, low1, up1, s1, low2, up2, xl, xr_hi, xr_lo, tr, trs, buf, send, recv, tsend, trecv, isem, osem):
     rows, slots, bs, _ = dens.shape
     pairs = rows // 2
     me = lax.axis_index("row")
@@ -75,10 +75,6 @@
         ref[p, blk(rb), blk(col)] = hi
         ref[p, blk(2 + rb), blk(col)] = lo
 
-    rq_hi[...] = jnp.zeros_like(rq_hi)
-    rq_lo[...] = jnp.zeros_like(rq_lo)
-    rz_hi[...] = jnp.zeros_like(rz_hi)
-    rz_lo[...] = jnp.zeros_like(rz_lo)
     mask[...] = jnp.zeros_like(mask)
     trs[...] = jnp.zeros_like(trs)
     eye = (lax.broadcasted_iota(jnp.int32, (bs, bs), 0) == lax.broadcasted_iota(jnp.int32, (bs, bs), 1)).astype(f32)
@@ -87,7 +83,6 @@
         return jnp.sum(x * eye, axis=0, keepdims=True)
 
     def load(p, total):
-        zero = jnp.zeros((bs, bs), jnp.bfloat16)
         fetch(p).wait()
         for rb in range(2):
             for s in range(slots):
@@ -96,31 +91,37 @@
                 mask[p, rb : rb + 1, blk(col)] = jnp.full((1, bs), 1.0, f32) * m
                 x = buf[2 * p + rb, s] * m
                 pf[p, blk(rb), blk(col)] = x
-                hi, lo = split(x)
+                if s == slots // 2:
+                    total = total + diag(x)
+        return total
+
+    def fill(p, carry):
+        zero = jnp.zeros((bs, bs), jnp.bfloat16)
+        for rb in range(2):
+            for s in range(slots):
+                col = s + rb
+                hi, lo = split(pf[p, blk(rb), blk(col)])
                 put_left(left, p, rb, col, hi, lo)
                 put_right(p, rb, col, hi, lo)
-                if s == slots // 2:
-                    total = total + diag(x)
             put_left(left, p, rb, 7 - 7 * rb, zero, zero)
-        return total
+        return carry
 
     trs[0:1, :] = lax.fori_loop(0, pairs, load, jnp.zeros((1, bs), f32))
 
     pl.semaphore_wait(barrier, n - 1)
     top = rows + 3
 
-    def halo_copies(src, low, up, first):
+    def halo_copies(src, low, up, triangle, base):
         nxt, prv = [], []
         for h in range(3):
             e = rows + h
             p, rb = divmod(e - 3, 2)
-            c0, c1 = (e, rows + 3) if first else (rows, e + 4)
+            c0, c1 = (e if triangle else rows), rows + 3
             nxt.append((src.at[p, blk(rb), pl.ds((c0 - 2 * p) * bs, (c1 - c0) * bs)], low[h]))
             e = 3 + h
             p, rb = divmod(e - 3, 2)
-            c0, c1 = (e, 6) if first else (e - 3, 6)
+            c0, c1 = (e if triangle else 3), 6
             prv.append((src.at[p, blk(rb), pl.ds((c0 - 2 * p) * bs, (c1 - c0) * bs)], up[h]))
-        base = 0 if first else 6
 
         def make(pairs_, off, dev):
             return [
@@ -158,8 +159,15 @@
             for c in prv:
                 c.wait_send()
 
-    first = halo_copies(pf, low0, up0, True)
+    first = halo_copies(pf, low0, up0, True, 0)
     start(first)
+
+    rq_hi[...] = jnp.zeros_like(rq_hi)
+    rq_lo[...] = jnp.zeros_like(rq_lo)
+    rz_hi[...] = jnp.zeros_like(rz_hi)
+    rz_lo[...] = jnp.zeros_like(rz_lo)
+    lax.fori_loop(0, pairs, fill, 0)
+
 
     def triple(a, b_hi, b_lo):
         y = dot(a, b_hi)
@@ -193,15 +201,15 @@
         lo, hi = max(0, 3 - 2 * p), min(8, rows + 3 - 2 * p)
         return lo + lo % 2, hi - hi % 2
 
-    def square_inner():
+    def square_inner(sf):
         for p in range(pairs):
             lo, hi = inner(p)
             for g in range(3):
                 k0, k1 = max(lo, spans[g][0]), min(hi, spans[g][1])
                 sf[p, :, (1 + 2 * g) * bs : (3 + 2 * g) * bs] = part(left, p, g, k0, k1)
 
-    def square_outer():
-        for p in range(pairs):
+    def square_outer(sf, order):
+        for p in order:
             lo, hi = inner(p)
             for g in range(3):
                 y = sf[p, :, (1 + 2 * g) * bs : (3 + 2 * g) * bs]
@@ -210,11 +218,11 @@
                 if hi < spans[g][1]:
                     y = y + part(left, p, g, hi, spans[g][1])
                 for rb, col, x in blocks(g, y):
-                    put_square(p, rb, col, x)
+                    put_square(sf, p, rb, col, x)
             for rb, col, x in corners(left, p):
-                put_square(p, rb, col, x)
-
-    def put_square(p, rb, col, y):
+                put_square(sf, p, rb, col, x)
+
+    def put_square(sf, p, rb, col, y):
         y = y * mask[p, rb : rb + 1, blk(col)]
         sf[p, blk(rb), blk(col)] = y
         put_left(cube_left, p, rb, col, *split(y))
@@ -224,7 +232,7 @@
         for rb in range(2):
             put_left(cube_left, p, rb, 7 - 7 * rb, zero, zero)
 
-    square_inner()
+    square_inner(s1)
 
     def own0(e, c):
         p, rb = divmod(e - 3, 2)
@@ -256,18 +264,22 @@
                 if c > h:
                     put_halo(top + c, top + h, x.T)
 
-    square_outer()
+    mid = halo_copies(s1, low2, up2, True, 12)
+    square_outer(s1, (0, pairs - 1))
+    start((mid[0][1:], mid[1][:2]))
+    square_outer(s1, range(1, pairs - 1))
+    start((mid[0][:1], mid[1][2:]))
 
     def cube(p, total):
         for rb, col, y in groups(cube_left, p):
-            x = 3.0 * sf[p, blk(rb), blk(col)] - 2.0 * (y * mask[p, rb : rb + 1, blk(col)])
+            x = 3.0 * s1[p, blk(rb), blk(col)] - 2.0 * (y * mask[p, rb : rb + 1, blk(col)])
             qf[p, blk(rb), blk(col)] = x
             put_left(left, p, rb, col, *split(x))
             if col == 3 + rb:
                 total = total + diag(x)
         return total
 
-    second = halo_copies(qf, low1, up1, False)
+    second = halo_copies(qf, low1, up1, False, 6)
     traced = cube(pairs - 1, cube(0, jnp.zeros((1, bs), f32)))
     start((second[0][1:], second[1][:2]))
     trs[1:2, :] = lax.fori_loop(1, pairs - 1, cube, traced)
@@ -281,14 +293,56 @@
 
     lax.fori_loop(0, pairs, refill, 0)
     start((second[0][:1], second[1][2:]))
-    square_inner()
+    square_inner(sf)
+
+    def cross(low):
+        own = [3, 4, 5] if low else [rows, rows + 1, rows + 2]
+        far = [0, 1, 2] if low else [top, top + 1, top + 2]
+        ks = far + own if low else own + far
+        copies, got = (mid[0], low2) if low else (mid[1], up2)
+        for h in range(3):
+            copies[h].wait_recv()
+        for i, k in enumerate(ks):
+            for h, j in enumerate(far):
+                if k in far:
+                    r, c = min(far.index(k), h), max(far.index(k), h)
+                    x = got[r][:, blk(c - r)]
+                    x = x if far.index(k) <= h else x.T
+                elif abs(k - j) <= 3:
+                    x = s1[(k - 3) // 2, blk((k - 3) % 2), blk(j - 2 * ((k - 3) // 2))]
+                else:
+                    x = jnp.zeros((bs, bs), f32)
+                xr_hi[blk(i), blk(h)], xr_lo[blk(i), blk(h)] = split(x)
+            for h, c in enumerate(own):
+                if abs(k - c) <= 3:
+                    x = pf[(c - 3) // 2, blk((c - 3) % 2), blk(k - 2 * ((c - 3) // 2))]
+                else:
+                    x = jnp.zeros((bs, bs), f32)
+                xl[blk(h), blk(i)], xl[blk(3 + h), blk(i)] = split(x)
+        y = dot(xl[...], xr_hi[...])
+        y = y[: 3 * bs] + y[3 * bs :] + dot(xl[: 3 * bs], xr_lo[...])
+        for i, c in enumerate(own):
+            p, rb = divmod(c - 3, 2)
+            for h, j in enumerate(far):
+                if abs(c - j) <= 3:
+                    col = j - 2 * p
+                    x = 3.0 * s1[p, blk(rb), blk(col)] - 2.0 * (y[blk(i), blk(h)] * mask[p, rb : rb + 1, blk(col)])
+                    put_halo(j, c, x.T)
 
     @pl.when(me > 0)
     def _():
+        cross(True)
+
+    @pl.when(me < n - 1)
+    def _():
+        cross(False)
+
+    @pl.when(me > 0)
+    def _():
         for h in range(3):
             second[0][h].wait_recv()
         for h in range(3):
-            for c in range(h + 4):
+            for c in range(3):
                 put_halo(h, c, low1[h][:, blk(c)])
 
     @pl.when(me < n - 1)
@@ -296,10 +350,10 @@
         for h in range(3):
             second[1][h].wait_recv()
         for h in range(3):
-            for c in range(rows + h, top + 3):
-                put_halo(top + h, c, up1[h][:, blk(c - rows - h)])
-
-    square_outer()
+            for c in range(3):
+                put_halo(top + h, top + c, up1[h][:, blk(c)])
+
+    square_outer(sf, range(pairs))
 
     def put_out(p, rb, col, y):
         x = 3.0 * sf[p, blk(rb), blk(col)] - 2.0 * (y * mask[p, rb : rb + 1, blk(col)])
@@ -327,6 +381,7 @@
 
     tr[me] = trs[...]
     wait_sends(first)
+    wait_sends(mid)
     wait_sends(second)
 
     @pl.loop(1, n)
@@ -376,13 +431,19 @@
             vm((pairs, 8, wide), f32),
             [vm((bs, (3 - h) * bs), f32) for h in range(3)],
             [vm((bs, (3 - h) * bs), f32) for h in range(3)],
-            [vm((bs, (4 + h) * bs), f32) for h in range(3)],
-            [vm((bs, (6 - h) * bs), f32) for h in range(3)],
+            [vm((bs, 3 * bs), f32) for h in range(3)],
+            [vm((bs, 3 * bs), f32) for h in range(3)],
+            vm((pairs, 2 * bs, wide), f32),
+            [vm((bs, (3 - h) * bs), f32) for h in range(3)],
+            [vm((bs, (3 - h) * bs), f32) for h in range(3)],
+            vm((6 * bs, 6 * bs), bf16),
+            vm((6 * bs, 3 * bs), bf16),
+            vm((6 * bs, 3 * bs), bf16),
             vm((n, 8, bs), f32),
             vm((8, bs), f32),
             vm(density.shape, f32),
-            pltpu.SemaphoreType.DMA((12,)),
-            pltpu.SemaphoreType.DMA((12,)),
+            pltpu.SemaphoreType.DMA((18,)),
+            pltpu.SemaphoreType.DMA((18,)),
             pltpu.SemaphoreType.DMA((n,)),
             pltpu.SemaphoreType.DMA((n,)),
             pltpu.SemaphoreType.DMA((pairs,)),

time: 59.5 us -> 55.1 us (0.926)
  Pallas kernels: 53.8 us -> 49.4 us
    pallas_call x1, Pallas kernels: 53.8 us -> 49.4 us  [on_device(): pl.pallas_call(functools.partial(kernel, n), out_shape=(jax.ShapeDtypeStr...]
where the time goes in v2:
time: 55.1 us; the launch traced here: 54.9 us
  Pallas kernels  49.4 us (90%)
  local copies, waits for them, and re-layouts  4.82 us (9%)
  between operations  0.65 us (1%)
    pallas_call x1, Pallas kernels, on_device(): pl.pallas_call(functools.partial(kernel, n), out_shape=(jax.ShapeDtypeStr...  49.4 us
    unnamed x4, local copies, waits for them, and re-layouts  4.82 us

profile of v2, /device:TPU:0, one launch (start us, length us, event | category | flops | bytes accessed | tf_op | source)
XLA Modules:
  0.0 54.9 jit_solution(7619938667767115622)
XLA Ops:
  0.6 49.4 %shard_map.41 = (f32[8,7,128,128]{3,2,1,0:T(8,128)}, f32[3]{0:T(128)}) custom-call(f32[8,7,128,128]{3,2,1,0:T(8,128)} %dens.1, s32[8,7]{1,0:T(8,128)} %cols.1), custom_call_target="tpu_custom_call" | custom-call | tf_op jit(solution)/shard_map/pallas_call | solution.py:416
  50.0 0.0 copy-start
  50.1 4.3 %copy.6 = f32[8,7,128,128]{3,2,1,0:T(8,128)} copy(f32[8,7,128,128]{3,2,1,0:T(8,128)} %get-tuple-element.4) | data formatting | bytes 7340032
  54.4 0.0 copy-done
  54.4 0.5 copy.7
Async XLA Ops:
  50.0 4.3 %copy-start = (f32[3]{0:T(128)S(1)}, f32[3]{0:T(128)}, u32[]{:S(2)}) copy-start(f32[3]{0:T(128)} %get-tuple-element.5) | copy-start | bytes 40

commit v3 on v2

--- a/solution.py
+++ b/solution.py
@@ -329,31 +329,18 @@
                     x = 3.0 * s1[p, blk(rb), blk(col)] - 2.0 * (y[blk(i), blk(h)] * mask[p, rb : rb + 1, blk(col)])
                     put_halo(j, c, x.T)
 
-    @pl.when(me > 0)
-    def _():
-        cross(True)
-
-    @pl.when(me < n - 1)
-    def _():
-        cross(False)
-
-    @pl.when(me > 0)
-    def _():
-        for h in range(3):
-            second[0][h].wait_recv()
-        for h in range(3):
-            for c in range(3):
-                put_halo(h, c, low1[h][:, blk(c)])
-
-    @pl.when(me < n - 1)
-    def _():
-        for h in range(3):
-            second[1][h].wait_recv()
-        for h in range(3):
-            for c in range(3):
-                put_halo(top + h, top + c, up1[h][:, blk(c)])
-
-    square_outer(sf, range(pairs))
+    def side(low):
+        @pl.when(me > 0 if low else me < n - 1)
+        def _():
+            cross(low)
+            copies, got, first_row = (second[0], low1, 0) if low else (second[1], up1, top)
+            for h in range(3):
+                copies[h].wait_recv()
+            for h in range(3):
+                for c in range(3):
+                    put_halo(first_row + h, first_row + c, got[h][:, blk(c)])
+
+        square_outer(sf, range(pairs // 2) if low else range(pairs // 2, pairs))
 
     def put_out(p, rb, col, y):
         x = 3.0 * sf[p, blk(rb), blk(col)] - 2.0 * (y * mask[p, rb : rb + 1, blk(col)])
@@ -367,13 +354,35 @@
                 total = total + diag(x)
         return total
 
-    trs[2:3, :] = lax.fori_loop(0, pairs, last, jnp.zeros((1, bs), f32))
-
     def rest(p, carry):
         for rb, col, y in groups(cube_left, p, (0, 2)):
             put_out(p, rb, col, y)
         return carry
 
+    def store(p):
+        return pltpu.make_async_copy(buf.at[pl.ds(2 * p, 2)], out.at[pl.ds(2 * p, 2)], osem.at[p])
+
+    def finish(low_first):
+        half = pairs // 2
+        a, b = ((0, half), (half, pairs)) if low_first else ((half, pairs), (0, half))
+        side(low_first)
+        total = lax.fori_loop(*a, last, jnp.zeros((1, bs), f32))
+        for p in range(*a):
+            rest(p, 0)
+            store(p).start()
+        side(not low_first)
+        trs[2:3, :] = lax.fori_loop(*b, last, total)
+
+    odd = lax.rem(me, 2)
+
+    @pl.when(odd == 0)
+    def _():
+        finish(False)
+
+    @pl.when(odd == 1)
+    def _():
+        finish(True)
+
     def trace_copy(k):
         return pltpu.make_async_remote_copy(
             src_ref=trs, dst_ref=tr.at[me], send_sem=tsend.at[k], recv_sem=trecv.at[k],
@@ -388,10 +397,8 @@
     def _(k):
         trace_copy(k).start()
 
-    def store(p):
-        return pltpu.make_async_copy(buf.at[pl.ds(2 * p, 2)], out.at[pl.ds(2 * p, 2)], osem.at[p])
-
-    for p in range(pairs):
+    for i in range(pairs // 2):
+        p = odd * (pairs // 2) + i
         rest(p, 0)
         store(p).start()
 

time: 55.1 us -> 52.2 us (0.947)
  Pallas kernels: 49.4 us -> 46.6 us
    pallas_call x1, Pallas kernels: 49.4 us -> 46.6 us  [on_device(): pl.pallas_call(functools.partial(kernel, n), out_shape=(jax.ShapeDtypeStr...]
where the time goes in v3:
time: 52.2 us; the launch traced here: 52 us
  Pallas kernels  46.6 us (89%)
  local copies, waits for them, and re-layouts  4.82 us (9%)
  between operations  0.65 us (1%)
    pallas_call x1, Pallas kernels, on_device(): pl.pallas_call(functools.partial(kernel, n), out_shape=(jax.ShapeDtypeStr...  46.6 us
    unnamed x4, local copies, waits for them, and re-layouts  4.82 us

profile of v3, /device:TPU:0, one launch (start us, length us, event | category | flops | bytes accessed | tf_op | source)
XLA Modules:
  0.0 52.0 jit_solution(1418479874275216593)
XLA Ops:
  0.6 46.6 %shard_map.41 = (f32[8,7,128,128]{3,2,1,0:T(8,128)}, f32[3]{0:T(128)}) custom-call(f32[8,7,128,128]{3,2,1,0:T(8,128)} %dens.1, s32[8,7]{1,0:T(8,128)} %cols.1), custom_call_target="tpu_custom_call" | custom-call | tf_op jit(solution)/shard_map/pallas_call | solution.py:423
  47.2 0.0 copy-start
  47.2 4.3 %copy.6 = f32[8,7,128,128]{3,2,1,0:T(8,128)} copy(f32[8,7,128,128]{3,2,1,0:T(8,128)} %get-tuple-element.4) | data formatting | bytes 7340032
  51.5 0.0 copy-done
  51.5 0.5 copy.7
Async XLA Ops:
  47.2 4.3 %copy-start = (f32[3]{0:T(128)S(1)}, f32[3]{0:T(128)}, u32[]{:S(2)}) copy-start(f32[3]{0:T(128)} %get-tuple-element.5) | copy-start | bytes 40
